TPU v7x, 768 devices: a whole 4x8x12 slice. The times are simulated.
768 devices in a mesh: seq: 64 (over x, y, core), head: 12 (over z).
Axes of the slice: x: 4, y: 8, z: 12, core: 2. Of those that a mesh axis runs over, the one named last changes fastest.
Arguments:
- queries: bfloat16 [32768, 3072], P('seq', 'head'), may hold values from -6 to 6
- key_feats: bfloat16 [32768, 3072], P('seq', 'head'), may hold values from -6 to 6
- value_feats: bfloat16 [32768, 3072], P('seq', 'head'), may hold values from -140 to 140
- targets: bfloat16 [32768, 3072], P('seq', 'head'), may hold values from -6 to 6
- norm_gain: float32 [3072], P('head'), may hold values from 0.5 to 1.5
- doc_lengths: int32 [20], replicated, may hold values from 1 to 8192, 32768 in all
Outputs:
- normed: bfloat16 [32768, 3072], P('seq', 'head')
- grad_queries: bfloat16 [32768, 3072], P('seq', 'head')
- grad_keys: bfloat16 [32768, 3072], P('seq', 'head')
- grad_values: bfloat16 [32768, 3072], P('seq', 'head')
Inputs may be any that keep to these rules, and one draw needn't show every extreme that they name: `doc_lengths`: lengths of the 20 documents packed in order into the 32768 positions; they sum to 32768 and the longest is exactly 8192.
All inputs are finite; a program needn't handle non-finite values.
Results may differ from a plain program's by a relative error of at most 0.015.
Values sent between devices are 32-bit elements; how exact they have to be, the bound alone decides.
A program may use at most 32 MiB of HBM per device.

v0:
```python
import jax
import jax.numpy as jnp
from jax import lax
from jax.sharding import PartitionSpec as P

DH = 128


def carried_in(x, axis, combine, identity, reverse):
    devices, position = (lax.axis_size(axis), lax.axis_index(axis))
    everything = jax.tree.map(lambda part: lax.all_gather(part, axis), x)
    start = jax.tree.map(
        lambda part, zero: jnp.broadcast_to(jnp.asarray(zero, part.dtype), part.shape), x, identity
    )

    def hop(k, before):
        at = devices - 1 - k if reverse else k
        reached = at > position if reverse else at < position
        new = combine(before, jax.tree.map(lambda part: part[at], everything))
        return jax.tree.map(lambda a, b: jnp.where(reached, a, b), new, before)

    return lax.fori_loop(0, devices, hop, start)


def document_ids(doc_lengths, positions):
    doc_ends = jnp.cumsum(doc_lengths, dtype=jnp.int32)
    return jnp.sum(
        (doc_ends[None, :] <= positions[:, None]).astype(jnp.int32), axis=1, dtype=jnp.int32
    )


def chain_combine(earlier, later):
    return (jnp.maximum(earlier[0], later[0]), later[1] + (1.0 - later[0]) * earlier[1])


def per_device(queries, key_feats, value_feats, targets, norm_gain, doc_lengths):
    tok_count = queries.shape[0]
    local_heads = queries.shape[1] // DH
    width_all = norm_gain.shape[0] * lax.axis_size("head")
    device = lax.axis_index("seq")
    offset = device * tok_count
    positions = offset + jnp.arange(tok_count, dtype=jnp.int32)
    edges = jnp.stack([offset - 1, offset + tok_count])
    token_docs = document_ids(doc_lengths, positions)
    edge_docs = document_ids(doc_lengths, edges)
    prev_doc = edge_docs[0]
    next_doc = edge_docs[1]
    first_doc = token_docs[0]
    last_doc = token_docs[-1]
    shape_three = (tok_count, local_heads, DH)
    query_three = queries.reshape(shape_three)
    key_three = key_feats.reshape(shape_three)
    value_three = value_feats.reshape(shape_three)
    gain_three = norm_gain.reshape(1, local_heads, DH)
    causal = jnp.arange(tok_count)[:, None] >= jnp.arange(tok_count)[None, :]
    same_doc = causal & (token_docs[:, None] == token_docs[None, :])
    use_in = (token_docs == prev_doc).astype(jnp.float32)[:, None, None]
    use_out = (token_docs == next_doc).astype(jnp.float32)[:, None, None]
    in_last = (token_docs == last_doc).astype(jnp.bfloat16)[:, None, None]
    in_first = (token_docs == first_doc).astype(jnp.bfloat16)[:, None, None]
    local_state = jnp.einsum(
        "thd,the->hde", key_three * in_last, value_three, preferred_element_type=jnp.float32
    )
    forward_flag = (last_doc != prev_doc).astype(jnp.float32)
    empty_state = jnp.zeros_like(local_state)
    carried = carried_in(
        (forward_flag, local_state),
        "seq",
        chain_combine,
        (jnp.zeros((), jnp.float32), empty_state),
        False,
    )
    carry_state = carried[1]
    carry_low = carry_state.astype(jnp.bfloat16)
    scores = jnp.einsum("thd,shd->hts", query_three, key_three, preferred_element_type=jnp.float32)
    attn = jnp.where(same_doc[None], scores, 0.0).astype(jnp.bfloat16)
    output = jnp.einsum("hts,she->the", attn, value_three, preferred_element_type=jnp.float32)
    output = output + use_in * jnp.einsum(
        "thd,hde->the", query_three, carry_low, preferred_element_type=jnp.float32
    )
    square_sum = lax.psum(jnp.sum(output * output, axis=(1, 2)), "head")
    inverse = lax.rsqrt(square_sum / width_all + 1e-06)[:, None, None]
    normed = (gain_three * output * inverse).astype(jnp.bfloat16)
    grad_normed = normed.astype(jnp.float32) - targets.reshape(shape_three).astype(jnp.float32)
    weighted = gain_three * grad_normed
    slope = lax.psum(jnp.sum(weighted * output, axis=(1, 2)), "head")[:, None, None]
    grad_output = (weighted * inverse - output * (slope * inverse**3 / width_all)).astype(
        jnp.bfloat16
    )
    tail_state = jnp.einsum(
        "thd,the->hde", query_three * in_first, grad_output, preferred_element_type=jnp.float32
    )
    reverse_flag = (first_doc != next_doc).astype(jnp.float32)
    suffixed = carried_in(
        (reverse_flag, tail_state),
        "seq",
        chain_combine,
        (jnp.zeros((), jnp.float32), empty_state),
        True,
    )
    suffix_low = suffixed[1].astype(jnp.bfloat16)
    mixing = jnp.einsum(
        "the,she->hts", grad_output, value_three, preferred_element_type=jnp.float32
    )
    mixing = jnp.where(same_doc[None], mixing, 0.0).astype(jnp.bfloat16)
    grad_q = jnp.einsum("hts,shd->thd", mixing, key_three, preferred_element_type=jnp.float32)
    grad_q = grad_q + use_in * jnp.einsum(
        "the,hde->thd", grad_output, carry_low, preferred_element_type=jnp.float32
    )
    grad_k = jnp.einsum("hts,thd->shd", mixing, query_three, preferred_element_type=jnp.float32)
    grad_k = grad_k + use_out * jnp.einsum(
        "she,hde->shd", value_three, suffix_low, preferred_element_type=jnp.float32
    )
    grad_v = jnp.einsum("hts,the->she", attn, grad_output, preferred_element_type=jnp.float32)
    grad_v = grad_v + use_out * jnp.einsum(
        "shd,hde->she", key_three, suffix_low, preferred_element_type=jnp.float32
    )
    flat_shape = (tok_count, local_heads * DH)
    return (
        normed.reshape(flat_shape),
        grad_q.astype(jnp.bfloat16).reshape(flat_shape),
        grad_k.astype(jnp.bfloat16).reshape(flat_shape),
        grad_v.astype(jnp.bfloat16).reshape(flat_shape),
    )


def solution(mesh):
    in_specs = (
        P("seq", "head"),
        P("seq", "head"),
        P("seq", "head"),
        P("seq", "head"),
        P("head"),
        P(),
    )
    out_specs = (P("seq", "head"), P("seq", "head"), P("seq", "head"), P("seq", "head"))
    return jax.shard_map(
        per_device, mesh=mesh, in_specs=in_specs, out_specs=out_specs, check_vma=False
    )
```

profile of v0, /device:TPU:1, one launch (start us, length us, event | category | flops | bytes accessed | tf_op | source)
XLA Modules:
  0.0 591.8 jit_solution(2104712529707716836)
XLA Ops:
  9.8 1.1 copy.134
  10.9 2.5 compare_convert_fusion
  16.9 1.1 copy.107
  18.2 1.3 dynamic-slice
  20.9 135.0 %all-reduce.2 = (f32[64]{0:T(128)S(1)}, f32[64]{0:T(128)}) all-reduce(f32[64]{0:T(128)S(1)} %dynamic-update-slice, f32[64]{0:T(128)S(1)} %dynamic-update-slice.1), channel_id=1, replica_groups=mesh['seq'=64,'head'=12] {'seq'}, use_global_device_ids=true, to_apply=%add | all-reduce | flops 128 | bytes 1024
  156.9 143.8 %while.30 = (s32[]{:T(128)}, f32[2,128,128]{2,1,0:T(8,128)S(1)}, s32[]{:T(128)}, f32[64,2,128,128]{3,2,1,0:T(8,128)}, f32[64]{0:T(128)S(1)}, /*index=5*/s32[]{:T(128)}, f32[1]{0:T(128)}, s32[]{:T(128)}) while((s32[]{:T(128)}, f32[2,128,128]{2,1,0:T(8,128)S(1)}, s32[]{:T(128)}, f32[64,2,128,128]{3,2,1,0:T(8,128)}, f32[64]{0:T(128)S(1)}, ...), condition=%wide.region_4.5_spmd.clone, body=%wide.region_3.4_spmd.clone.sunk | while | flops 131077 | bytes 393361 | solution.py:22
  158.1 1.0 fusion.59
  162.6 1.0 fusion.59
  164.8 1.0 fusion.59
  167.1 1.0 fusion.59
  171.6 1.0 fusion.59
  173.8 1.0 fusion.59
  176.1 1.0 fusion.59
  180.6 1.0 fusion.59
  182.8 1.0 fusion.59
  301.5 19.5 %psum.14 = f32[512]{0:T(512)S(1)} all-reduce(f32[512]{0:T(512)S(1)} %get-tuple-element.316), channel_id=1, replica_groups=mesh['seq'=64,'head'=12] {'head'}, use_global_device_ids=true, to_apply=%region_6.7 | all-reduce | flops 512 | bytes 4096 | tf_op jit(solution)/shard_map/psum | solution.py:81
  321.2 15.4 %psum.15 = f32[512]{0:T(512)S(1)} all-reduce(f32[512]{0:T(512)S(1)} %multiply_reduce_fusion), channel_id=1, replica_groups=mesh['seq'=64,'head'=12] {'head'}, use_global_device_ids=true, to_apply=%region_8.9 | all-reduce | flops 512 | bytes 4096 | tf_op jit(solution)/shard_map/psum | solution.py:86
  339.5 1.5 select_convert_fusion
  341.0 2.1 fusion.8
  343.1 1.8 copy.99
  344.9 91.2 %all-gather.7.cloned.1.call-done = f32[128,128,128]{2,1,0:T(8,128)} async-done(((f32[2,128,128]{2,1,0:T(8,128)}), f32[128,128,128]{2,1,0:T(8,128)}) %all-gather.7.cloned.1.call-update) | async-done | bytes 8388624 | tf_op jit(solution)/shard_map/all_gather | solution.py:11
  436.1 144.2 %while.31 = (s32[]{:T(128)}, f32[2,128,128]{2,1,0:T(8,128)S(1)}, s32[]{:T(128)}, f32[64,2,128,128]{3,2,1,0:T(8,128)}, f32[64]{0:T(128)S(1)}, /*index=5*/s32[]{:T(128)}, s32[]{:T(128)}, s32[]{:T(128)}, s32[]{:T(128)}, f32[1]{0:T(128)}) while((s32[]{:T(128)}, f32[2,128,128]{2,1,0:T(8,128)S(1)}, s32[]{:T(128)}, ...), condition=%wide.region_10.11_spmd.clone, body=%wide.region_9.10_spmd.clone.sunk | while | flops 131081 | bytes 393423 | solution.py:22
  580.3 1.0 fusion.5
  582.8 1.3 fusion.9
  (298 shorter events, 204.6 us)
Async XLA Ops:
  7.2 6.2 %copy-start = (bf16[512,256]{1,0:T(8,128)(2,1)S(1)}, bf16[512,256]{1,0:T(8,128)(2,1)}, u32[]{:S(2)}) copy-start(bf16[512,256]{1,0:T(8,128)(2,1)} %param.12) | copy-start | bytes 786436
  7.2 149.0 %copy-start.1 = (bf16[512,256]{1,0:T(8,128)(2,1)S(1)}, bf16[512,256]{1,0:T(8,128)(2,1)}, u32[]{:S(2)}) copy-start(bf16[512,256]{1,0:T(8,128)(2,1)} %param.11) | copy-start | bytes 786436
  7.2 10.8 %copy-start.3 = (bf16[512,256]{1,0:T(8,128)(2,1)S(1)}, bf16[512,256]{1,0:T(8,128)(2,1)}, u32[]{:S(2)}) copy-start(bf16[512,256]{1,0:T(8,128)(2,1)} %param.13) | copy-start | bytes 786436
  7.2 149.5 %all-gather.5.cloned.1.call-start = ((), (), s32[]{:S(2)}) async-start(), calls=%async_computation | async-start | bytes 8519680 | tf_op jit(solution)/shard_map/all_gather | solution.py:11
  10.9 6.0 %copy-start.2 = (bf16[512,256]{0,1:T(8,128)(2,1)}, bf16[512,256]{0,1:T(8,128)(2,1)S(1)}, u32[]{:S(2)}) copy-start(bf16[512,256]{0,1:T(8,128)(2,1)S(1)} %copy.134) | copy-start | bytes 786436
  14.3 421.8 %all-gather.7.cloned.1.call-start = ((), (), s32[]{:S(2)}) async-start(), calls=%async_computation.1 | async-start | bytes 8519680 | tf_op jit(solution)/shard_map/all_gather | solution.py:11
  156.1 0.7 copy-start.4
  300.7 20.3 %copy-start.5 = (f32[256]{0:T(256)S(1)}, f32[256]{0:T(256)}, u32[]{:S(2)}) copy-start(f32[256]{0:T(256)} %param.14) | copy-start | bytes 3076
  339.5 96.7 %copy-start.6 = (f32[64]{0:T(128)S(1)}, f32[64]{0:T(128)}, u32[]{:S(2)}) copy-start(f32[64]{0:T(128)} %get-tuple-element.408) | copy-start | bytes 772
Sparse Core Ops, SparseCore 0:
  14.4 101.7 all-gather.4
  338.5 97.5 all-gather.6
where the time goes:
time: 596 us; the launch traced here: 592 us
  blocking collectives  170 us (29%)
  other arithmetic  131 us (22%)
  waiting for transfers between devices  91.3 us (15%)
  loops' own time  86.7 us (15%)
  local copies, waits for them, and re-layouts  86.6 us (15%)
  between operations  16.8 us (3%)
  matrix products  9.86 us (2%)
    unnamed x1, blocking collectives  135 us
    select_n x128, other arithmetic, hop(): return jax.tree.map(lambda a, b: jnp.where(reached, a, b), new, before)  126 us
    all_gather x2, waiting for transfers between devices, carried_in(): everything = jax.tree.map(lambda part: lax.all_gather(part, axis), x)  91.2 us
    another operation x2, loops' own time, carried_in(): return lax.fori_loop(0, devices, hop, start)  86.7 us
    dynamic_slice x128, local copies, waits for them, and re-layouts, hop(): new = combine(before, jax.tree.map(lambda part: part[at], everything))  75.1 us
    psum x1, blocking collectives, per_device(): square_sum = lax.psum(jnp.sum(output * output, axis=(1, 2)), 'head')  19.5 us
    psum x1, blocking collectives, per_device(): lax.psum(jnp.sum(weighted * output, axis=(1, 2)), 'head')[:, None, None]  15.4 us
  transfers between devices with their start and end apart: 2, of which 1 were waited for; matrix products, arithmetic and copies ran while one was open for 2% of the time, Pallas kernels for 0%

commit v1 on v0

v1 whole, which is shorter than its diff:
```python
import functools

import jax
import jax.numpy as jnp
from jax import lax
from jax.experimental import pallas as pl
from jax.experimental.pallas import tpu as pltpu
from jax.sharding import PartitionSpec as P

DH = 128
MAXDOC = 8192
MESH = pl.DeviceIdType.MESH
F32 = jnp.float32
BF16 = jnp.bfloat16


def contract(a, b, dims):
    return lax.dot_general(a, b, (dims, ((), ())), preferred_element_type=F32)


NN = ((1,), (0,))
NT = ((1,), (1,))
TN = ((0,), (0,))


def kernel(
    seqs, ring, zs, len_ref,
    q_ref, k_ref, v_ref, t_ref, g_ref,
    normed_ref, gq_ref, gk_ref, gv_ref,
    flag_ref, loc_ref, gat_ref, tot_ref, totin_ref, car_ref, carin_ref,
    attn_ref, mix_ref, out_ref, go_ref, sums_ref, sumsin_ref,
    ssem, rsem, tsem, zsend, zrecv,
):
    tok, width = q_ref.shape
    heads = width // DH
    width_all = width * zs
    groups = seqs // ring
    docs = len_ref.shape[0]
    device = lax.axis_index("seq")
    z = lax.axis_index("head")
    place = lax.rem(device, ring)
    group = device // ring
    base = group * ring
    after = lax.rem(device + ring, seqs)
    before = lax.rem(device + seqs - ring, seqs)

    barrier = pltpu.get_barrier_semaphore()

    def greet_ring(i, carry):
        pl.semaphore_signal(
            barrier, inc=1, device_id=(base + lax.rem(place + i, ring), z), device_id_type=MESH
        )
        return carry

    def greet_heads(i, carry):
        pl.semaphore_signal(
            barrier, inc=1, device_id=(device, lax.rem(z + i, zs)), device_id_type=MESH
        )
        return carry

    lax.fori_loop(1, ring, greet_ring, 0)
    pl.semaphore_signal(barrier, inc=1, device_id=(after, z), device_id_type=MESH)
    pl.semaphore_signal(barrier, inc=1, device_id=(before, z), device_id_type=MESH)
    lax.fori_loop(1, zs, greet_heads, 0)

    ends = []
    total = jnp.int32(0)
    for d in range(docs):
        total = total + len_ref[d]
        ends.append(total)
    first = device * tok
    last = first + tok - 1
    far = jnp.int32(2**30)
    start_last = jnp.int32(0)
    start_next = jnp.int32(0)
    end_first = far
    end_prev = far
    for e in ends:
        start_last = jnp.where(e <= last, e, start_last)
        start_next = jnp.where(e <= last + 1, e, start_next)
    for e in reversed(ends):
        end_first = jnp.where(e > first, e, end_first)
        end_prev = jnp.where(e > first - 1, e, end_prev)

    def per_row(shape):
        return first + lax.broadcasted_iota(jnp.int32, shape, 0)

    row_pos = per_row((tok, DH))
    in_last = row_pos >= start_last
    in_first = row_pos < end_first
    use_in = row_pos < end_prev
    use_out = row_pos >= start_next

    def head(ref, h):
        return ref[:, h * DH : (h + 1) * DH]

    def keep(mask, x):
        return jnp.where(mask, x.astype(F32), 0.0)

    slices = heads * DH // ring

    def put_state(which, h, state):
        per_head = DH // slices
        loc_ref[which, h * per_head : (h + 1) * per_head] = state.reshape(per_head, slices, DH)

    for h in range(heads):
        put_state(0, h, contract(keep(in_last, head(k_ref, h)).astype(BF16), head(v_ref, h), TN))

    block_first = (base + lax.broadcasted_iota(jnp.int32, (ring, DH), 0)) * tok
    cut_f = jnp.zeros((ring, DH), jnp.int32)
    cut_r = jnp.zeros((ring, DH), jnp.int32)
    for e in ends:
        cut_f = cut_f | jnp.where((e >= block_first) & (e < block_first + tok), 1, 0)
        cut_r = cut_r | jnp.where((e > block_first) & (e <= block_first + tok), 1, 0)
    flag_ref[0] = 1.0 - cut_f.astype(F32)
    flag_ref[1] = 1.0 - cut_r.astype(F32)

    column_pos = first + lax.broadcasted_iota(jnp.int32, (1, tok), 1)
    end_of = jnp.full((1, tok), far, jnp.int32)
    for e in reversed(ends):
        end_of = jnp.where(e > column_pos, e, end_of)
    tall = per_row((tok, tok))
    wide = first + lax.broadcasted_iota(jnp.int32, (tok, tok), 1)
    same_doc = (tall >= wide) & (tall < end_of)

    def slice_copy(which, stage, i):
        src, dst = ((loc_ref, gat_ref), (car_ref, carin_ref))[stage]
        peer = lax.rem(place + i, ring)
        return pltpu.make_async_remote_copy(
            src_ref=src.at[which, peer],
            dst_ref=dst.at[which, place],
            send_sem=ssem.at[which, stage, i],
            recv_sem=rsem.at[which, stage, i],
            device_id=(base + peer, z),
            device_id_type=MESH,
        )

    def start_slices(which, stage):
        def one(i, carry):
            slice_copy(which, stage, i).start()
            return carry

        lax.fori_loop(1, ring, one, 0)

    def wait_slices(which, stage):
        def one(i, carry):
            slice_copy(which, stage, i).wait()
            return carry

        lax.fori_loop(1, ring, one, 0)

    def total_copy(which):
        return pltpu.make_async_remote_copy(
            src_ref=tot_ref.at[which],
            dst_ref=totin_ref.at[which],
            send_sem=tsem.at[which, 0],
            recv_sem=tsem.at[which, 1],
            device_id=(before if which else after, z),
            device_id_type=MESH,
        )

    def order(which):
        return reversed(range(ring)) if which else range(ring)

    def gather_states(which):
        gat_ref[which, place] = loc_ref[which, place]
        start_slices(which, 0)

    def fold_column(which):
        wait_slices(which, 0)
        run = jnp.zeros((slices, DH), F32)
        for j in order(which):
            run = gat_ref[which, j] + flag_ref[which, j : j + 1] * run
        tot_ref[which] = run
        total_copy(which).start()

    def hand_out(which):
        total_copy(which).wait()
        inside = group < groups - 1 if which else group > 0
        run = jnp.where(inside, totin_ref[which], 0.0)
        for j in order(which):
            car_ref[which, j] = run
            run = gat_ref[which, j] + flag_ref[which, j : j + 1] * run
        carin_ref[which, place] = car_ref[which, place]
        start_slices(which, 1)

    def take_state(which, h):
        per_head = DH // slices
        part = carin_ref[which, h * per_head : (h + 1) * per_head]
        return part.reshape(DH, DH).astype(BF16)

    def attend(h):
        scores = contract(head(q_ref, h), head(k_ref, h), NT)
        attn_ref[h] = jnp.where(same_doc, scores, 0.0).astype(BF16)

    def local_output(h):
        out_ref[:, h * DH : (h + 1) * DH] = contract(attn_ref[h], head(v_ref, h), NN)

    pl.semaphore_wait(barrier, ring + zs)
    gather_states(0)
    for h in range(heads):
        attend(h)
    for h in range(heads):
        local_output(h)
    fold_column(0)
    hand_out(0)
    wait_slices(0, 1)

    gain = g_ref[...]
    squares = jnp.zeros((tok, 1), F32)
    gained = jnp.zeros((tok, 1), F32)
    crossed = jnp.zeros((tok, 1), F32)
    for h in range(heads):
        out = head(out_ref, h) + keep(use_in, contract(head(q_ref, h), take_state(0, h), NN))
        out_ref[:, h * DH : (h + 1) * DH] = out
        scaled = gain[:, h * DH : (h + 1) * DH] * out
        squares = squares + jnp.sum(out * out, axis=1, keepdims=True)
        gained = gained + jnp.sum(scaled * scaled, axis=1, keepdims=True)
        crossed = crossed + jnp.sum(scaled * head(t_ref, h).astype(F32), axis=1, keepdims=True)
    lane = lax.broadcasted_iota(jnp.int32, (tok, DH), 1)
    packed = jnp.where(lane == 0, squares, jnp.where(lane == 1, gained, crossed))
    sums_ref[...] = packed.T[0 : sums_ref.shape[0]]
    sumsin_ref[z] = sums_ref[...]

    def sum_copy(i):
        return pltpu.make_async_remote_copy(
            src_ref=sums_ref,
            dst_ref=sumsin_ref.at[z],
            send_sem=zsend.at[i],
            recv_sem=zrecv.at[i],
            device_id=(device, lax.rem(z + i, zs)),
            device_id_type=MESH,
        )

    def start_sum(i, carry):
        sum_copy(i).start()
        return carry

    def wait_sum(i, carry):
        sum_copy(i).wait()
        return carry

    lax.fori_loop(1, zs, start_sum, 0)
    lax.fori_loop(1, zs, wait_sum, 0)
    summed = sumsin_ref[0]
    for i in range(1, zs):
        summed = summed + sumsin_ref[i]
    inverse_row = lax.rsqrt(summed[0:1] / width_all + 1e-06)
    slope_row = inverse_row * summed[1:2] - summed[2:3]
    pull_row = slope_row * (inverse_row * inverse_row * inverse_row) / width_all
    inverse = jnp.broadcast_to(inverse_row, (DH, tok)).T
    pull = jnp.broadcast_to(pull_row, (DH, tok)).T
    for h in range(heads):
        cols = slice(h * DH, (h + 1) * DH)
        out = out_ref[:, cols]
        gain_h = gain[:, cols]
        normed = (gain_h * out * inverse).astype(BF16)
        normed_ref[:, cols] = normed
        weighted = gain_h * (normed.astype(F32) - t_ref[:, cols].astype(F32))
        grad = (weighted * inverse - out * pull).astype(BF16)
        go_ref[:, cols] = grad
        put_state(1, h, contract(keep(in_first, head(q_ref, h)).astype(BF16), grad, TN))
    gather_states(1)

    def mix(h):
        mixing = contract(head(go_ref, h), head(v_ref, h), NT)
        mix_ref[h] = jnp.where(same_doc, mixing, 0.0).astype(BF16)

    def query_grad(h):
        far_part = contract(head(go_ref, h), take_state(0, h), NT)
        near = contract(mix_ref[h], head(k_ref, h), NN)
        gq_ref[:, h * DH : (h + 1) * DH] = (near + keep(use_in, far_part)).astype(BF16)

    def near_grads(h):
        return (
            contract(mix_ref[h], head(q_ref, h), TN),
            contract(attn_ref[h], head(go_ref, h), TN),
        )

    for h in range(heads):
        mix(h)
        query_grad(h)
    fold_column(1)
    hand_out(1)
    near = [near_grads(h) for h in range(heads)]
    wait_slices(1, 1)
    for h in range(heads):
        suffix = take_state(1, h)
        cols = slice(h * DH, (h + 1) * DH)
        far_k = contract(head(v_ref, h), suffix, NT)
        far_v = contract(head(k_ref, h), suffix, NN)
        gk_ref[:, cols] = (near[h][0] + keep(use_out, far_k)).astype(BF16)
        gv_ref[:, cols] = (near[h][1] + keep(use_out, far_v)).astype(BF16)


def solution(mesh):
    seqs, zs = mesh.shape["seq"], mesh.shape["head"]

    def per_device(queries, key_feats, value_feats, targets, norm_gain, doc_lengths):
        tok, width = queries.shape
        ring = MAXDOC // tok
        heads = width // DH
        slices = width // ring
        states = pltpu.VMEM((2, ring, slices, DH), F32)
        vmem = pl.BlockSpec(memory_space=pltpu.VMEM)
        return tuple(
            pl.pallas_call(
                functools.partial(kernel, seqs, ring, zs),
                out_shape=[jax.ShapeDtypeStruct((tok, width), BF16)] * 4,
                in_specs=[pl.BlockSpec(memory_space=pltpu.SMEM)] + [vmem] * 5,
                out_specs=[vmem] * 4,
                scratch_shapes=[
                    pltpu.VMEM((2, ring, DH), F32),
                    states,
                    states,
                    pltpu.VMEM((2, slices, DH), F32),
                    pltpu.VMEM((2, slices, DH), F32),
                    states,
                    states,
                    pltpu.VMEM((heads, tok, tok), BF16),
                    pltpu.VMEM((heads, tok, tok), BF16),
                    pltpu.VMEM((tok, width), F32),
                    pltpu.VMEM((tok, width), BF16),
                    pltpu.VMEM((4, tok), F32),
                    pltpu.VMEM((zs, 4, tok), F32),
                    pltpu.SemaphoreType.DMA((2, 2, ring)),
                    pltpu.SemaphoreType.DMA((2, 2, ring)),
                    pltpu.SemaphoreType.DMA((2, 2)),
                    pltpu.SemaphoreType.DMA((zs,)),
                    pltpu.SemaphoreType.DMA((zs,)),
                ],
                compiler_params=pltpu.CompilerParams(collective_id=0, has_side_effects=True),
            )(
                doc_lengths,
                queries,
                key_feats,
                value_feats,
                targets,
                norm_gain.reshape(1, width),
            )
        )

    spec = P("seq", "head")
    return jax.shard_map(
        per_device,
        mesh=mesh,
        in_specs=(spec, spec, spec, spec, P("head"), P()),
        out_specs=(spec, spec, spec, spec),
        check_vma=False,
    )
```

time: 596 us -> 64.3 us (0.11)
  blocking collectives: 170 us -> 0 us
  other arithmetic: 131 us -> 0 us
  waiting for transfers between devices: 91.3 us -> 0 us
  loops' own time: 86.7 us -> 0 us
  local copies, waits for them, and re-layouts: 86.6 us -> 4.5 us
  Pallas kernels: 0 us -> 58.8 us
  between operations: 16.8 us -> 0.65 us
  matrix products: 9.86 us -> 0 us
    unnamed x1 -> x0, blocking collectives: 135 us -> none
    select_n x128 -> x0, other arithmetic: 126 us -> none  [hop(): return jax.tree.map(lambda a, b: jnp.where(reached, a, b), new, before)]
    all_gather x2 -> x0, waiting for transfers between devices: 91.2 us -> none  [carried_in(): everything = jax.tree.map(lambda part: lax.all_gather(part, axis), x)]
    another operation x2 -> x0, loops' own time: 86.7 us -> none  [carried_in(): return lax.fori_loop(0, devices, hop, start)]
    dynamic_slice x128 -> x0, local copies, waits for them, and re-layouts: 75.1 us -> none  [hop(): new = combine(before, jax.tree.map(lambda part: part[at], everything))]
    pallas_call x0 -> x1, Pallas kernels: none -> 58.8 us  [per_device(): pl.pallas_call(functools.partial(kernel, seqs, ring, zs), out_shape=[jax....]
    psum x2 -> x0, blocking collectives: 34.9 us -> none  [the longest x1 19.5 us: per_device(): square_sum = lax.psum(jnp.sum(output * output, axis=(1, 2)), 'head')]
    dot_general x12 -> x0, matrix products: 9.86 us -> none  [the longest x1 2.13 us: per_device(): jnp.einsum('hts,shd->thd', mixing, key_three, preferred_element_type=jnp....]
  transfers between devices with their start and end apart: 2 -> 0, of which waited for: 1 -> 0; matrix products, arithmetic and copies ran while one was open for 2% -> 0% of each run, Pallas kernels for 0% -> 0%
where the time goes in v1:
time: 64.3 us; the launch traced here: 63.9 us
  Pallas kernels  58.8 us (91%)
  local copies, waits for them, and re-layouts  4.5 us (7%)
  between operations  0.65 us (1%)
    pallas_call x1, Pallas kernels, per_device(): pl.pallas_call(functools.partial(kernel, seqs, ring, zs), out_shape=[jax....  58.8 us
    unnamed x10, local copies, waits for them, and re-layouts  4.5 us

profile of v1, /device:TPU:1, one launch (start us, length us, event | category | flops | bytes accessed | tf_op | source)
XLA Modules:
  0.0 63.9 jit_solution(12126399841958784844)
XLA Ops:
  0.6 58.8 %shard_map.93 = (bf16[512,256]{1,0:T(8,128)(2,1)}, bf16[512,256]{1,0:T(8,128)(2,1)}, bf16[512,256]{1,0:T(8,128)(2,1)}, bf16[512,256]{1,0:T(8,128)(2,1)}) custom-call(s32[20]{0:T(128)} %len_ref.1, bf16[512,256]{1,0:T(8,128)(2,1)} %q_ref.1, bf16[512,256]{1,0:T(8,128)(2,1)} %k_ref.1, bf16[512,256]{1,0:T(8,128)(2,1)} %v_ref.1, bf16[512,256]{1,0:T(8,128)(2,1)} %t_ref.1, ...), custom_call_target="tpu_custom_call" | custom-call | tf_op jit(solution)/shard_map/pallas_call | solution.py:307
  59.4 0.0 copy-start.2
  59.4 1.7 %copy.14 = bf16[512,256]{1,0:T(8,128)(2,1)} copy(bf16[512,256]{1,0:T(8,128)(2,1)} %get-tuple-element.8) | data formatting | bytes 524288
  61.1 0.0 copy-done.2
  61.1 0.0 copy-start.1
  61.1 0.7 %copy.15 = bf16[512,256]{1,0:T(8,128)(2,1)} copy(bf16[512,256]{1,0:T(8,128)(2,1)S(1)} %copy-done.2) | data formatting | bytes 524288
  61.8 0.3 copy-done.1
  62.2 0.0 copy-start
  62.2 0.7 %copy.16 = bf16[512,256]{1,0:T(8,128)(2,1)} copy(bf16[512,256]{1,0:T(8,128)(2,1)S(1)} %copy-done.1) | data formatting | bytes 524288
  62.9 0.3 copy-done
  63.2 0.7 %copy.17 = bf16[512,256]{1,0:T(8,128)(2,1)} copy(bf16[512,256]{1,0:T(8,128)(2,1)S(1)} %copy-done) | data formatting | bytes 524288
Async XLA Ops:
  59.4 1.7 %copy-start.2 = (bf16[512,256]{1,0:T(8,128)(2,1)S(1)}, bf16[512,256]{1,0:T(8,128)(2,1)}, u32[]{:S(2)}) copy-start(bf16[512,256]{1,0:T(8,128)(2,1)} %get-tuple-element.9) | copy-start | bytes 786436
  61.1 1.0 %copy-start.1 = (bf16[512,256]{1,0:T(8,128)(2,1)S(1)}, bf16[512,256]{1,0:T(8,128)(2,1)}, u32[]{:S(2)}) copy-start(bf16[512,256]{1,0:T(8,128)(2,1)} %get-tuple-element.10) | copy-start | bytes 786436
  62.2 1.0 %copy-start = (bf16[512,256]{1,0:T(8,128)(2,1)S(1)}, bf16[512,256]{1,0:T(8,128)(2,1)}, u32[]{:S(2)}) copy-start(bf16[512,256]{1,0:T(8,128)(2,1)} %get-tuple-element.11) | copy-start | bytes 786436

commit v2 on v1

--- a/solution.py
+++ b/solution.py
@@ -23,16 +23,21 @@
 TN = ((0,), (0,))
 
 
+def far_first(n):
+    return sorted(range(1, n), key=lambda i: -min(i, n - i))
+
+
 def kernel(
-    seqs, ring, zs, len_ref,
-    q_ref, k_ref, v_ref, t_ref, g_ref,
+    seqs, ring, zs, len_in,
+    q_in, k_in, v_in, t_in, g_in,
     normed_ref, gq_ref, gk_ref, gv_ref,
-    flag_ref, loc_ref, gat_ref, tot_ref, totin_ref, car_ref, carin_ref,
+    len_ref, q_ref, k_ref, v_ref, t_ref, g_ref, flag_ref, loc_ref, gat_ref, tot_ref, totin_ref, car_ref, carin_ref,
     attn_ref, mix_ref, out_ref, go_ref, sums_ref, sumsin_ref,
-    ssem, rsem, tsem, zsend, zrecv,
+    load_sem, ssem, rsem, tsem, zsend, zrecv,
 ):
     tok, width = q_ref.shape
     heads = width // DH
+    rows = tok // DH
     width_all = width * zs
     groups = seqs // ring
     docs = len_ref.shape[0]
@@ -46,22 +51,33 @@
 
     barrier = pltpu.get_barrier_semaphore()
 
-    def greet_ring(i, carry):
+    for i in far_first(zs):
+        pl.semaphore_signal(
+            barrier, inc=1, device_id=(device, lax.rem(z + i, zs)), device_id_type=MESH
+        )
+    for i in far_first(ring):
         pl.semaphore_signal(
             barrier, inc=1, device_id=(base + lax.rem(place + i, ring), z), device_id_type=MESH
         )
-        return carry
-
-    def greet_heads(i, carry):
-        pl.semaphore_signal(
-            barrier, inc=1, device_id=(device, lax.rem(z + i, zs)), device_id_type=MESH
-        )
-        return carry
-
-    lax.fori_loop(1, ring, greet_ring, 0)
     pl.semaphore_signal(barrier, inc=1, device_id=(after, z), device_id_type=MESH)
     pl.semaphore_signal(barrier, inc=1, device_id=(before, z), device_id_type=MESH)
-    lax.fori_loop(1, zs, greet_heads, 0)
+
+    loads = [
+        pltpu.make_async_copy(src, dst, load_sem.at[i])
+        for i, (src, dst) in enumerate(
+            (
+                (len_in, len_ref),
+                (k_in, k_ref),
+                (v_in, v_ref),
+                (q_in, q_ref),
+                (t_in, t_ref),
+                (g_in, g_ref),
+            )
+        )
+    ]
+    for load in loads:
+        load.start()
+    loads[0].wait()
 
     ends = []
     total = jnp.int32(0)
@@ -103,6 +119,8 @@
         per_head = DH // slices
         loc_ref[which, h * per_head : (h + 1) * per_head] = state.reshape(per_head, slices, DH)
 
+    loads[1].wait()
+    loads[2].wait()
     for h in range(heads):
         put_state(0, h, contract(keep(in_last, head(k_ref, h)).astype(BF16), head(v_ref, h), TN))
 
@@ -136,11 +154,8 @@
         )
 
     def start_slices(which, stage):
-        def one(i, carry):
+        for i in far_first(ring):
             slice_copy(which, stage, i).start()
-            return carry
-
-        lax.fori_loop(1, ring, one, 0)
 
     def wait_slices(which, stage):
         def one(i, carry):
@@ -198,6 +213,9 @@
 
     pl.semaphore_wait(barrier, ring + zs)
     gather_states(0)
+    loads[3].wait()
+    loads[4].wait()
+    loads[5].wait()
     for h in range(heads):
         attend(h)
     for h in range(heads):
@@ -207,19 +225,30 @@
     wait_slices(0, 1)
 
     gain = g_ref[...]
-    squares = jnp.zeros((tok, 1), F32)
-    gained = jnp.zeros((tok, 1), F32)
-    crossed = jnp.zeros((tok, 1), F32)
+    squares = jnp.zeros((tok, DH), F32)
+    gained = jnp.zeros((tok, DH), F32)
+    crossed = jnp.zeros((tok, DH), F32)
     for h in range(heads):
         out = head(out_ref, h) + keep(use_in, contract(head(q_ref, h), take_state(0, h), NN))
         out_ref[:, h * DH : (h + 1) * DH] = out
         scaled = gain[:, h * DH : (h + 1) * DH] * out
-        squares = squares + jnp.sum(out * out, axis=1, keepdims=True)
-        gained = gained + jnp.sum(scaled * scaled, axis=1, keepdims=True)
-        crossed = crossed + jnp.sum(scaled * head(t_ref, h).astype(F32), axis=1, keepdims=True)
+        squares = squares + out * out
+        gained = gained + scaled * scaled
+        crossed = crossed + scaled * head(t_ref, h).astype(F32)
     lane = lax.broadcasted_iota(jnp.int32, (tok, DH), 1)
-    packed = jnp.where(lane == 0, squares, jnp.where(lane == 1, gained, crossed))
-    sums_ref[...] = packed.T[0 : sums_ref.shape[0]]
+    packed = jnp.where(
+        lane == 0,
+        jnp.sum(squares, axis=1, keepdims=True),
+        jnp.where(
+            lane == 1,
+            jnp.sum(gained, axis=1, keepdims=True),
+            jnp.sum(crossed, axis=1, keepdims=True),
+        ),
+    )
+    for c in range(rows):
+        turned = packed[c * DH : (c + 1) * DH].T
+        for r in range(3):
+            sums_ref[r * rows + c : r * rows + c + 1] = turned[r : r + 1]
     sumsin_ref[z] = sums_ref[...]
 
     def sum_copy(i):
@@ -232,24 +261,24 @@
             device_id_type=MESH,
         )
 
-    def start_sum(i, carry):
+    for i in far_first(zs):
         sum_copy(i).start()
-        return carry
-
-    def wait_sum(i, carry):
+    for i in range(1, zs):
         sum_copy(i).wait()
-        return carry
-
-    lax.fori_loop(1, zs, start_sum, 0)
-    lax.fori_loop(1, zs, wait_sum, 0)
     summed = sumsin_ref[0]
     for i in range(1, zs):
         summed = summed + sumsin_ref[i]
-    inverse_row = lax.rsqrt(summed[0:1] / width_all + 1e-06)
-    slope_row = inverse_row * summed[1:2] - summed[2:3]
-    pull_row = slope_row * (inverse_row * inverse_row * inverse_row) / width_all
-    inverse = jnp.broadcast_to(inverse_row, (DH, tok)).T
-    pull = jnp.broadcast_to(pull_row, (DH, tok)).T
+    inverse_rows = lax.rsqrt(summed[0:rows] / width_all + 1e-06)
+    slope_rows = inverse_rows * summed[rows : 2 * rows] - summed[2 * rows : 3 * rows]
+    pull_rows = slope_rows * (inverse_rows * inverse_rows * inverse_rows) / width_all
+
+    def upright(x):
+        return jnp.concatenate(
+            [jnp.broadcast_to(x[c : c + 1], (DH, DH)).T for c in range(rows)], axis=0
+        )
+
+    inverse = upright(inverse_rows)
+    pull = upright(pull_rows)
     for h in range(heads):
         cols = slice(h * DH, (h + 1) * DH)
         out = out_ref[:, cols]
@@ -293,6 +322,16 @@
         gv_ref[:, cols] = (near[h][1] + keep(use_out, far_v)).astype(BF16)
 
 
+def flush(*refs):
+    *arrays, sem = refs
+    n = len(arrays) // 2
+    copies = [pltpu.make_async_copy(arrays[i], arrays[n + i], sem.at[i]) for i in range(n)]
+    for copy in copies:
+        copy.start()
+    for copy in copies:
+        copy.wait()
+
+
 def solution(mesh):
     seqs, zs = mesh.shape["seq"], mesh.shape["head"]
 
@@ -303,13 +342,21 @@
         slices = width // ring
         states = pltpu.VMEM((2, ring, slices, DH), F32)
         vmem = pl.BlockSpec(memory_space=pltpu.VMEM)
-        return tuple(
+        hbm = pl.BlockSpec(memory_space=pltpu.HBM)
+        block = pltpu.VMEM((tok, width), BF16)
+        held = (
             pl.pallas_call(
                 functools.partial(kernel, seqs, ring, zs),
-                out_shape=[jax.ShapeDtypeStruct((tok, width), BF16)] * 4,
-                in_specs=[pl.BlockSpec(memory_space=pltpu.SMEM)] + [vmem] * 5,
+                out_shape=[pltpu.VMEM((tok, width), BF16)] * 4,
+                in_specs=[hbm] * 6,
                 out_specs=[vmem] * 4,
                 scratch_shapes=[
+                    pltpu.SMEM(doc_lengths.shape, jnp.int32),
+                    block,
+                    block,
+                    block,
+                    block,
+                    pltpu.VMEM((1, width), F32),
                     pltpu.VMEM((2, ring, DH), F32),
                     states,
                     states,
@@ -321,23 +368,41 @@
                     pltpu.VMEM((heads, tok, tok), BF16),
                     pltpu.VMEM((tok, width), F32),
                     pltpu.VMEM((tok, width), BF16),
-                    pltpu.VMEM((4, tok), F32),
-                    pltpu.VMEM((zs, 4, tok), F32),
+                    pltpu.VMEM((3 * tok // DH, DH), F32),
+                    pltpu.VMEM((zs, 3 * tok // DH, DH), F32),
+                    pltpu.SemaphoreType.DMA((6,)),
                     pltpu.SemaphoreType.DMA((2, 2, ring)),
                     pltpu.SemaphoreType.DMA((2, 2, ring)),
                     pltpu.SemaphoreType.DMA((2, 2)),
                     pltpu.SemaphoreType.DMA((zs,)),
                     pltpu.SemaphoreType.DMA((zs,)),
                 ],
-                compiler_params=pltpu.CompilerParams(collective_id=0, has_side_effects=True),
+                compiler_params=pltpu.CompilerParams(
+                    collective_id=0, has_side_effects=True, vmem_limit_bytes=40 * 2**20
+                ),
             )(
-                doc_lengths,
-                queries,
-                key_feats,
-                value_feats,
-                targets,
-                norm_gain.reshape(1, width),
+                *(
+                    pltpu.with_memory_space_constraint(x, pltpu.HBM)
+                    for x in (
+                        doc_lengths,
+                        queries,
+                        key_feats,
+                        value_feats,
+                        targets,
+                        norm_gain.reshape(1, width),
+                    )
+                )
             )
+        )
+        return tuple(
+            pl.pallas_call(
+                flush,
+                out_shape=[jax.ShapeDtypeStruct((tok, width), BF16)] * 4,
+                in_specs=[vmem] * 4,
+                out_specs=[hbm] * 4,
+                scratch_shapes=[pltpu.SemaphoreType.DMA((4,))],
+                compiler_params=pltpu.CompilerParams(vmem_limit_bytes=8 * 2**20),
+            )(*held)
         )
 
     spec = P("seq", "head")

time: 64.3 us -> 56.1 us (0.87)
  local copies, waits for them, and re-layouts: 4.5 us -> 0 us
  Pallas kernels: 58.8 us -> 55 us
    unnamed x10 -> x0, local copies, waits for them, and re-layouts: 4.5 us -> none
    pallas_call x1 -> x2, Pallas kernels: 58.8 us -> 55 us  [the longest x1 54 us: per_device(): pl.pallas_call(functools.partial(kernel, seqs, ring, zs), out_shape=[pltp...]
where the time goes in v2:
time: 56.1 us; the launch traced here: 55.6 us
  Pallas kernels  55 us (98%)
  between operations  0.64 us (1%)
    pallas_call x1, Pallas kernels, per_device(): pl.pallas_call(functools.partial(kernel, seqs, ring, zs), out_shape=[pltp...  54 us

profile of v2, /device:TPU:1, one launch (start us, length us, event | category | flops | bytes accessed | tf_op | source)
XLA Modules:
  0.0 55.6 jit_solution(17123567480898340337)
XLA Ops:
  0.6 54.0 %shard_map.93 = (bf16[512,256]{1,0:T(8,128)(2,1)S(1)}, bf16[512,256]{1,0:T(8,128)(2,1)S(1)}, bf16[512,256]{1,0:T(8,128)(2,1)S(1)}, bf16[512,256]{1,0:T(8,128)(2,1)S(1)}) custom-call(s32[20]{0:T(128)} %len_in.1, bf16[512,256]{1,0:T(8,128)(2,1)} %q_in.1, bf16[512,256]{1,0:T(8,128)(2,1)} %k_in.1, bf16[512,256]{1,0:T(8,128)(2,1)} %v_in.1, ...), custom_call_target="tpu_custom_call" | custom-call | tf_op jit(solution)/shard_map/pallas_call | solution.py:348
  54.6 1.0 %shard_map.94 = (bf16[512,256]{1,0:T(8,128)(2,1)}, bf16[512,256]{1,0:T(8,128)(2,1)}, bf16[512,256]{1,0:T(8,128)(2,1)}, bf16[512,256]{1,0:T(8,128)(2,1)}) custom-call(bf16[512,256]{1,0:T(8,128)(2,1)S(1)} %get-tuple-element.8.refs_0_, bf16[512,256]{1,0:T(8,128)(2,1)S(1)} %get-tuple-element.9.refs_1_, bf16[512,256]{1,0:T(8,128)(2,1)S(1)} %get-tuple-element.10.refs_2_, ...), custom_call_target="tpu_custom_call" | custom-call | tf_op jit(solution)/shard_map/pallas_call | solution.py:398

commit v3 on v2

--- a/solution.py
+++ b/solution.py
@@ -31,7 +31,7 @@
     seqs, ring, zs, len_in,
     q_in, k_in, v_in, t_in, g_in,
     normed_ref, gq_ref, gk_ref, gv_ref,
-    len_ref, q_ref, k_ref, v_ref, t_ref, g_ref, flag_ref, loc_ref, gat_ref, tot_ref, totin_ref, car_ref, carin_ref,
+    len_ref, q_ref, k_ref, v_ref, t_ref, g_ref, flag_ref, through_ref, loc_ref, gat_ref, pre_ref, tot_ref, totin_ref, car_ref, carin_ref,
     attn_ref, mix_ref, out_ref, go_ref, sums_ref, sumsin_ref,
     load_sem, ssem, rsem, tsem, zsend, zrecv,
 ):
@@ -158,8 +158,12 @@
             slice_copy(which, stage, i).start()
 
     def wait_slices(which, stage):
+        for i in reversed(far_first(ring)):
+            slice_copy(which, stage, i).wait_recv()
+
+    def wait_sent(which, stage):
         def one(i, carry):
-            slice_copy(which, stage, i).wait()
+            slice_copy(which, stage, i).wait_send()
             return carry
 
         lax.fori_loop(1, ring, one, 0)
@@ -178,26 +182,32 @@
         return reversed(range(ring)) if which else range(ring)
 
     def gather_states(which):
+        start_slices(which, 0)
         gat_ref[which, place] = loc_ref[which, place]
-        start_slices(which, 0)
 
     def fold_column(which):
         wait_slices(which, 0)
         run = jnp.zeros((slices, DH), F32)
         for j in order(which):
+            pre_ref[which, j] = run
             run = gat_ref[which, j] + flag_ref[which, j : j + 1] * run
         tot_ref[which] = run
         total_copy(which).start()
+        through = jnp.ones((1, DH), F32)
+        for j in order(which):
+            through_ref[which, j : j + 1] = through
+            through = through * flag_ref[which, j : j + 1]
 
     def hand_out(which):
-        total_copy(which).wait()
+        total_copy(which).wait_recv()
         inside = group < groups - 1 if which else group > 0
         run = jnp.where(inside, totin_ref[which], 0.0)
-        for j in order(which):
-            car_ref[which, j] = run
-            run = gat_ref[which, j] + flag_ref[which, j : j + 1] * run
+        for j in range(ring):
+            car_ref[which, j] = pre_ref[which, j] + through_ref[which, j : j + 1] * run
+        start_slices(which, 1)
         carin_ref[which, place] = car_ref[which, place]
-        start_slices(which, 1)
+        total_copy(which).wait_send()
+        wait_sent(which, 0)
 
     def take_state(which, h):
         per_head = DH // slices
@@ -263,8 +273,9 @@
 
     for i in far_first(zs):
         sum_copy(i).start()
-    for i in range(1, zs):
-        sum_copy(i).wait()
+    wait_sent(0, 1)
+    for i in reversed(far_first(zs)):
+        sum_copy(i).wait_recv()
     summed = sumsin_ref[0]
     for i in range(1, zs):
         summed = summed + sumsin_ref[i]
@@ -312,6 +323,8 @@
     fold_column(1)
     hand_out(1)
     near = [near_grads(h) for h in range(heads)]
+    for i in range(1, zs):
+        sum_copy(i).wait_send()
     wait_slices(1, 1)
     for h in range(heads):
         suffix = take_state(1, h)
@@ -320,6 +333,7 @@
         far_v = contract(head(k_ref, h), suffix, NN)
         gk_ref[:, cols] = (near[h][0] + keep(use_out, far_k)).astype(BF16)
         gv_ref[:, cols] = (near[h][1] + keep(use_out, far_v)).astype(BF16)
+    wait_sent(1, 1)
 
 
 def flush(*refs):
@@ -358,6 +372,8 @@
                     block,
                     pltpu.VMEM((1, width), F32),
                     pltpu.VMEM((2, ring, DH), F32),
+                    pltpu.VMEM((2, ring, DH), F32),
+                    states,
                     states,
                     states,
                     pltpu.VMEM((2, slices, DH), F32),

time: 56.1 us -> 56 us (level)
  no operation moved by 1% of the time
where the time goes in v3:
time: 56 us; the launch traced here: 55.4 us
  Pallas kernels  54.8 us (98%)
  between operations  0.64 us (1%)
    pallas_call x1, Pallas kernels, per_device(): pl.pallas_call(functools.partial(kernel, seqs, ring, zs), out_shape=[pltp...  53.8 us

profile of v3, /device:TPU:1, one launch (start us, length us, event | category | flops | bytes accessed | tf_op | source)
XLA Modules:
  0.0 55.4 jit_solution(7307795681359540807)
XLA Ops:
  0.6 53.8 %shard_map.93 = (bf16[512,256]{1,0:T(8,128)(2,1)S(1)}, bf16[512,256]{1,0:T(8,128)(2,1)S(1)}, bf16[512,256]{1,0:T(8,128)(2,1)S(1)}, bf16[512,256]{1,0:T(8,128)(2,1)S(1)}) custom-call(s32[20]{0:T(128)} %len_in.1, bf16[512,256]{1,0:T(8,128)(2,1)} %q_in.1, bf16[512,256]{1,0:T(8,128)(2,1)} %k_in.1, bf16[512,256]{1,0:T(8,128)(2,1)} %v_in.1, ...), custom_call_target="tpu_custom_call" | custom-call | tf_op jit(solution)/shard_map/pallas_call | solution.py:362
  54.4 1.0 %shard_map.94 = (bf16[512,256]{1,0:T(8,128)(2,1)}, bf16[512,256]{1,0:T(8,128)(2,1)}, bf16[512,256]{1,0:T(8,128)(2,1)}, bf16[512,256]{1,0:T(8,128)(2,1)}) custom-call(bf16[512,256]{1,0:T(8,128)(2,1)S(1)} %get-tuple-element.8.refs_0_, bf16[512,256]{1,0:T(8,128)(2,1)S(1)} %get-tuple-element.9.refs_1_, bf16[512,256]{1,0:T(8,128)(2,1)S(1)} %get-tuple-element.10.refs_2_, ...), custom_call_target="tpu_custom_call" | custom-call | tf_op jit(solution)/shard_map/pallas_call | solution.py:414

commit v4 on v3

--- a/solution.py
+++ b/solution.py
@@ -32,7 +32,7 @@
     q_in, k_in, v_in, t_in, g_in,
     normed_ref, gq_ref, gk_ref, gv_ref,
     len_ref, q_ref, k_ref, v_ref, t_ref, g_ref, flag_ref, through_ref, loc_ref, gat_ref, pre_ref, tot_ref, totin_ref, car_ref, carin_ref,
-    attn_ref, mix_ref, out_ref, go_ref, sums_ref, sumsin_ref,
+    turned_ref, attn_ref, mix_ref, out_ref, go_ref, sums_ref, sumsin_ref,
     load_sem, ssem, rsem, tsem, zsend, zrecv,
 ):
     tok, width = q_ref.shape
@@ -49,19 +49,6 @@
     after = lax.rem(device + ring, seqs)
     before = lax.rem(device + seqs - ring, seqs)
 
-    barrier = pltpu.get_barrier_semaphore()
-
-    for i in far_first(zs):
-        pl.semaphore_signal(
-            barrier, inc=1, device_id=(device, lax.rem(z + i, zs)), device_id_type=MESH
-        )
-    for i in far_first(ring):
-        pl.semaphore_signal(
-            barrier, inc=1, device_id=(base + lax.rem(place + i, ring), z), device_id_type=MESH
-        )
-    pl.semaphore_signal(barrier, inc=1, device_id=(after, z), device_id_type=MESH)
-    pl.semaphore_signal(barrier, inc=1, device_id=(before, z), device_id_type=MESH)
-
     loads = [
         pltpu.make_async_copy(src, dst, load_sem.at[i])
         for i, (src, dst) in enumerate(
@@ -77,6 +64,20 @@
     ]
     for load in loads:
         load.start()
+
+    barrier = pltpu.get_barrier_semaphore()
+
+    for i in far_first(zs):
+        pl.semaphore_signal(
+            barrier, inc=1, device_id=(device, lax.rem(z + i, zs)), device_id_type=MESH
+        )
+    for i in far_first(ring):
+        pl.semaphore_signal(
+            barrier, inc=1, device_id=(base + lax.rem(place + i, ring), z), device_id_type=MESH
+        )
+    pl.semaphore_signal(barrier, inc=1, device_id=(after, z), device_id_type=MESH)
+    pl.semaphore_signal(barrier, inc=1, device_id=(before, z), device_id_type=MESH)
+
     loads[0].wait()
 
     ends = []
@@ -178,6 +179,9 @@
             device_id_type=MESH,
         )
 
+    def gives(which):
+        return group > 0 if which else group < groups - 1
+
     def order(which):
         return reversed(range(ring)) if which else range(ring)
 
@@ -192,21 +196,35 @@
             pre_ref[which, j] = run
             run = gat_ref[which, j] + flag_ref[which, j : j + 1] * run
         tot_ref[which] = run
-        total_copy(which).start()
+
+        @pl.when(gives(which))
+        def _():
+            total_copy(which).start()
+
         through = jnp.ones((1, DH), F32)
         for j in order(which):
             through_ref[which, j : j + 1] = through
             through = through * flag_ref[which, j : j + 1]
 
     def hand_out(which):
-        total_copy(which).wait_recv()
-        inside = group < groups - 1 if which else group > 0
-        run = jnp.where(inside, totin_ref[which], 0.0)
+        @pl.when(gives(1 - which))
+        def _():
+            total_copy(which).wait_recv()
+
+        @pl.when(jnp.logical_not(gives(1 - which)))
+        def _():
+            totin_ref[which] = jnp.zeros((slices, DH), F32)
+
+        run = totin_ref[which]
         for j in range(ring):
             car_ref[which, j] = pre_ref[which, j] + through_ref[which, j : j + 1] * run
         start_slices(which, 1)
         carin_ref[which, place] = car_ref[which, place]
-        total_copy(which).wait_send()
+
+        @pl.when(gives(which))
+        def _():
+            total_copy(which).wait_send()
+
         wait_sent(which, 0)
 
     def take_state(which, h):
@@ -274,6 +292,8 @@
     for i in far_first(zs):
         sum_copy(i).start()
     wait_sent(0, 1)
+    for h in range(heads):
+        turned_ref[h] = keep(in_first, head(q_ref, h)).T.astype(BF16)
     for i in reversed(far_first(zs)):
         sum_copy(i).wait_recv()
     summed = sumsin_ref[0]
@@ -299,7 +319,7 @@
         weighted = gain_h * (normed.astype(F32) - t_ref[:, cols].astype(F32))
         grad = (weighted * inverse - out * pull).astype(BF16)
         go_ref[:, cols] = grad
-        put_state(1, h, contract(keep(in_first, head(q_ref, h)).astype(BF16), grad, TN))
+        put_state(1, h, contract(turned_ref[h], grad, NN))
     gather_states(1)
 
     def mix(h):
@@ -380,6 +400,7 @@
                     pltpu.VMEM((2, slices, DH), F32),
                     states,
                     states,
+                    pltpu.VMEM((heads, DH, tok), BF16),
                     pltpu.VMEM((heads, tok, tok), BF16),
                     pltpu.VMEM((heads, tok, tok), BF16),
                     pltpu.VMEM((tok, width), F32),

time: 56 us -> 55.4 us (0.989)
  no operation moved by 1% of the time
where the time goes in v4:
time: 55.4 us; the launch traced here: 55.3 us
  Pallas kernels  54.6 us (99%)
  between operations  0.64 us (1%)
    pallas_call x1, Pallas kernels, per_device(): pl.pallas_call(functools.partial(kernel, seqs, ring, zs), out_shape=[pltp...  53.6 us

profile of v4, /device:TPU:1, one launch (start us, length us, event | category | flops | bytes accessed | tf_op | source)
XLA Modules:
  0.0 55.3 jit_solution(14775115049494026538)
XLA Ops:
  0.6 53.6 %shard_map.93 = (bf16[512,256]{1,0:T(8,128)(2,1)S(1)}, bf16[512,256]{1,0:T(8,128)(2,1)S(1)}, bf16[512,256]{1,0:T(8,128)(2,1)S(1)}, bf16[512,256]{1,0:T(8,128)(2,1)S(1)}) custom-call(s32[20]{0:T(128)} %len_in.1, bf16[512,256]{1,0:T(8,128)(2,1)} %q_in.1, bf16[512,256]{1,0:T(8,128)(2,1)} %k_in.1, bf16[512,256]{1,0:T(8,128)(2,1)} %v_in.1, ...), custom_call_target="tpu_custom_call" | custom-call | tf_op jit(solution)/shard_map/pallas_call | solution.py:382
  54.3 1.0 %shard_map.94 = (bf16[512,256]{1,0:T(8,128)(2,1)}, bf16[512,256]{1,0:T(8,128)(2,1)}, bf16[512,256]{1,0:T(8,128)(2,1)}, bf16[512,256]{1,0:T(8,128)(2,1)}) custom-call(bf16[512,256]{1,0:T(8,128)(2,1)S(1)} %get-tuple-element.8.refs_0_, bf16[512,256]{1,0:T(8,128)(2,1)S(1)} %get-tuple-element.9.refs_1_, bf16[512,256]{1,0:T(8,128)(2,1)S(1)} %get-tuple-element.10.refs_2_, ...), custom_call_target="tpu_custom_call" | custom-call | tf_op jit(solution)/shard_map/pallas_call | solution.py:435

commit v5 on v4

--- a/solution.py
+++ b/solution.py
@@ -263,20 +263,10 @@
         squares = squares + out * out
         gained = gained + scaled * scaled
         crossed = crossed + scaled * head(t_ref, h).astype(F32)
-    lane = lax.broadcasted_iota(jnp.int32, (tok, DH), 1)
-    packed = jnp.where(
-        lane == 0,
-        jnp.sum(squares, axis=1, keepdims=True),
-        jnp.where(
-            lane == 1,
-            jnp.sum(gained, axis=1, keepdims=True),
-            jnp.sum(crossed, axis=1, keepdims=True),
-        ),
-    )
-    for c in range(rows):
-        turned = packed[c * DH : (c + 1) * DH].T
-        for r in range(3):
-            sums_ref[r * rows + c : r * rows + c + 1] = turned[r : r + 1]
+    for r, terms in enumerate((squares, gained, crossed)):
+        for c in range(rows):
+            turned = terms[c * DH : (c + 1) * DH].T
+            sums_ref[r * rows + c : r * rows + c + 1] = jnp.sum(turned, axis=0, keepdims=True)
     sumsin_ref[z] = sums_ref[...]
 
     def sum_copy(i):

time: 55.4 us -> 55.2 us (level)
  no operation moved by 1% of the time
where the time goes in v5:
time: 55.2 us; the launch traced here: 55 us
  Pallas kernels  54.4 us (99%)
  between operations  0.64 us (1%)
    pallas_call x1, Pallas kernels, per_device(): pl.pallas_call(functools.partial(kernel, seqs, ring, zs), out_shape=[pltp...  53.4 us

profile of v5, /device:TPU:1, one launch (start us, length us, event | category | flops | bytes accessed | tf_op | source)
XLA Modules:
  0.0 55.0 jit_solution(14281615350853016282)
XLA Ops:
  0.6 53.4 %shard_map.93 = (bf16[512,256]{1,0:T(8,128)(2,1)S(1)}, bf16[512,256]{1,0:T(8,128)(2,1)S(1)}, bf16[512,256]{1,0:T(8,128)(2,1)S(1)}, bf16[512,256]{1,0:T(8,128)(2,1)S(1)}) custom-call(s32[20]{0:T(128)} %len_in.1, bf16[512,256]{1,0:T(8,128)(2,1)} %q_in.1, bf16[512,256]{1,0:T(8,128)(2,1)} %k_in.1, bf16[512,256]{1,0:T(8,128)(2,1)} %v_in.1, ...), custom_call_target="tpu_custom_call" | custom-call | tf_op jit(solution)/shard_map/pallas_call | solution.py:372
  54.0 1.0 %shard_map.94 = (bf16[512,256]{1,0:T(8,128)(2,1)}, bf16[512,256]{1,0:T(8,128)(2,1)}, bf16[512,256]{1,0:T(8,128)(2,1)}, bf16[512,256]{1,0:T(8,128)(2,1)}) custom-call(bf16[512,256]{1,0:T(8,128)(2,1)S(1)} %get-tuple-element.8.refs_0_, bf16[512,256]{1,0:T(8,128)(2,1)S(1)} %get-tuple-element.9.refs_1_, bf16[512,256]{1,0:T(8,128)(2,1)S(1)} %get-tuple-element.10.refs_2_, ...), custom_call_target="tpu_custom_call" | custom-call | tf_op jit(solution)/shard_map/pallas_call | solution.py:425
